TPU v7x, 256 devices: a whole 4x4x8 slice. The times are simulated.
256 devices in a mesh: dp: 64 (over z, y, core), tensor: 4 (over x).
Axes of the slice: x: 4, y: 4, z: 8, core: 2. Of those that a mesh axis runs over, the one named last changes fastest.
Arguments:
- queries: bfloat16 [32768, 2048], P('dp', 'tensor'), may hold values from -360 to 360
- neighbours: int32 [512, 2], P('dp'), may hold values from 0 to 63, as said below
- counts: int32 [512], P('dp'), may hold values from 1 to 2
- states: bfloat16 [64, 128, 4096], P('dp'), may hold values from -6 to 6
- w_key: bfloat16 [4096, 2048], P('dp', 'tensor'), may hold values from -0.09375 to 0.09375
- w_value: bfloat16 [4096, 2048], P('dp', 'tensor'), may hold values from -0.09375 to 0.09375
- cotangent: bfloat16 [32768, 2048], P('dp', 'tensor'), may hold values from -6 to 6
Outputs:
- context: bfloat16 [32768, 2048], P('dp', 'tensor')
- query_grad: bfloat16 [32768, 2048], P('dp', 'tensor')
- state_grad: bfloat16 [64, 128, 4096], P('dp', None, 'tensor')
Inputs may be any that keep to these rules, and one draw needn't show every extreme that they name: Neighbour n is held by dp index n. Among the 16 slots of one index of dp, at most 1 name neighbours of one holder, and some holder is named exactly 1 times.
All inputs are finite; a program needn't handle non-finite values.
Results may differ from a plain program's by a relative error of at most 0.035.
The roundings to bfloat16 on the way count: a program that leaves them out, or rounds other values in their place, can miss the bound.
Values may be sent and summed in bfloat16 or wider, within the bound.
A program may use at most 128 MiB of HBM per device.

v0:
```python
import math

import jax
import jax.numpy as jnp
from jax import lax
from jax.sharding import PartitionSpec as P

HEAD = 128


def local(queries, neighbours, counts, states, w_key, w_value, cotangent):
    dp_count = lax.axis_size("dp")
    spans, neigh = neighbours.shape
    slots = spans * neigh
    capacity = (slots + dp_count - 1) // dp_count
    buffer_rows = dp_count * capacity
    nbr_dev, nbr_len, dmodel = states.shape
    local_width = queries.shape[1]
    heads_here = local_width // HEAD
    span_len = queries.shape[0] // spans
    score_scale = 1.0 / math.sqrt(HEAD)
    slot_ids = neighbours.reshape(slots)
    holder = slot_ids // nbr_dev
    slot_order = jnp.arange(slots, dtype=jnp.int32)
    earlier = (holder[:, None] == holder[None, :]) & (slot_order[None, :] < slot_order[:, None])
    holder_rank = jnp.sum(earlier.astype(jnp.int32), axis=1)
    position = holder * capacity + holder_rank
    placing = position[None, :] == jnp.arange(buffer_rows, dtype=jnp.int32)[:, None]
    place_half = placing.astype(jnp.bfloat16)
    place_full = placing.astype(jnp.float32)
    query_spans = queries.reshape(spans, 1, span_len * local_width)
    query_slots = jnp.broadcast_to(query_spans, (spans, neigh, span_len * local_width)).reshape(
        slots, span_len * local_width
    )
    send_query = jnp.dot(place_half, query_slots, preferred_element_type=jnp.float32).astype(
        jnp.bfloat16
    )
    send_query = send_query.reshape(dp_count, capacity, span_len, local_width)
    flat_states = states.reshape(nbr_dev * nbr_len, dmodel)
    key_full = lax.all_gather(w_key, "dp", axis=0, tiled=True)
    value_full = lax.all_gather(w_value, "dp", axis=0, tiled=True)
    key_acc = jnp.dot(flat_states, key_full, preferred_element_type=jnp.float32)
    value_acc = jnp.dot(flat_states, value_full, preferred_element_type=jnp.float32)
    key_rows = key_acc.astype(jnp.bfloat16).reshape(nbr_len, heads_here, HEAD)
    value_rows = value_acc.astype(jnp.bfloat16).reshape(nbr_len, heads_here, HEAD)
    key_rows, value_rows, key_full, value_full = (key_rows, value_rows, key_full, value_full)
    recv_query = lax.all_to_all(send_query, "dp", split_axis=0, concat_axis=0, tiled=True)
    lead = recv_query.shape[:-1]
    item_query = recv_query.reshape(lead + (heads_here, HEAD))
    scores = (
        jnp.einsum("abqhd,khd->abqhk", item_query, key_rows, preferred_element_type=jnp.float32)
        * score_scale
    )
    row_max = jnp.max(scores, axis=-1, keepdims=True)
    log_total = row_max[..., 0] + jnp.log(jnp.sum(jnp.exp(scores - row_max), axis=-1))
    prob_out = jnp.exp(scores - log_total[..., None])
    part_out = jnp.einsum(
        "abqhk,khd->abqhd",
        prob_out.astype(jnp.bfloat16),
        value_rows,
        preferred_element_type=jnp.float32,
    ).astype(jnp.bfloat16)
    item_part = part_out.reshape(lead + (local_width,))
    item_query = recv_query.reshape(dp_count, capacity, span_len, heads_here, HEAD)
    prob_half = prob_out.astype(jnp.bfloat16)
    back_part, back_log = (
        lax.all_to_all(
            item_part.astype(jnp.float32), "dp", split_axis=0, concat_axis=0, tiled=True
        ).astype(item_part.dtype),
        lax.all_to_all(log_total, "dp", split_axis=0, concat_axis=0, tiled=True),
    )
    back_part = back_part.reshape(buffer_rows, span_len, local_width)
    back_log = back_log.reshape(buffer_rows, span_len, heads_here)
    got_part = back_part[position].reshape(spans, neigh, span_len, heads_here, HEAD)
    got_log = back_log[position].reshape(spans, neigh, span_len, heads_here)
    is_valid = jnp.arange(neigh, dtype=jnp.int32)[None, :] < counts[:, None]
    live = is_valid[:, :, None, None]
    masked = jnp.where(live, got_log, -1e30)
    top_part = jnp.max(masked, axis=1, keepdims=True)
    raw_weight = jnp.where(live, jnp.exp(masked - top_part), 0.0)
    mix_weight = raw_weight / jnp.sum(raw_weight, axis=1, keepdims=True)
    part_full = got_part.astype(jnp.float32)
    mixed_rows = jnp.sum(mix_weight[..., None] * part_full, axis=1)
    context = mixed_rows.astype(jnp.bfloat16).reshape(spans * span_len, local_width)
    grad_rows = cotangent.astype(jnp.float32).reshape(spans, span_len, heads_here, HEAD)
    part_grad = lax.optimization_barrier(
        (mix_weight[..., None] * grad_rows[:, None]).astype(jnp.bfloat16)
    )
    lse_grad = mix_weight * jnp.sum(grad_rows[:, None] * (part_full - mixed_rows[:, None]), axis=-1)
    rest_term = jnp.sum(part_grad.astype(jnp.float32) * part_full, axis=-1) - lse_grad
    send_grad = jnp.dot(
        place_half,
        part_grad.reshape(slots, span_len * local_width),
        preferred_element_type=jnp.float32,
    ).astype(jnp.bfloat16)
    send_grad = send_grad.reshape(dp_count, capacity, span_len, local_width)
    send_rest = jnp.dot(
        place_full, rest_term.reshape(slots, span_len * heads_here), precision=lax.Precision.HIGHEST
    )
    send_rest = send_rest.reshape(dp_count, capacity, span_len, heads_here)
    recv_grad, recv_rest = (
        lax.all_to_all(
            send_grad.astype(jnp.float32), "dp", split_axis=0, concat_axis=0, tiled=True
        ).astype(send_grad.dtype),
        lax.all_to_all(send_rest, "dp", split_axis=0, concat_axis=0, tiled=True),
    )
    item_grad = recv_grad.reshape(dp_count, capacity, span_len, heads_here, HEAD)
    dprob = jnp.einsum(
        "abqhd,khd->abqhk", item_grad, value_rows, preferred_element_type=jnp.float32
    )
    dscore = prob_out * (dprob - recv_rest[..., None])
    dscore_half = dscore.astype(jnp.bfloat16)
    item_dq = (
        jnp.einsum("abqhk,khd->abqhd", dscore_half, key_rows, preferred_element_type=jnp.float32)
        * score_scale
    )
    item_dq = item_dq.astype(jnp.bfloat16).reshape(dp_count, capacity, span_len, local_width)
    back_dq = lax.all_to_all(item_dq, "dp", split_axis=0, concat_axis=0, tiled=True)
    key_grad = (
        jnp.einsum("abqhk,abqhd->khd", dscore_half, item_query, preferred_element_type=jnp.float32)
        * score_scale
    )
    key_grad = key_grad.astype(jnp.bfloat16).reshape(nbr_dev * nbr_len, local_width)
    value_grad = jnp.einsum(
        "abqhk,abqhd->khd", prob_half, item_grad, preferred_element_type=jnp.float32
    )
    value_grad = value_grad.astype(jnp.bfloat16).reshape(nbr_dev * nbr_len, local_width)
    contract = (((1,), (1,)), ((), ()))
    state_term = lax.dot_general(key_grad, key_full, contract, preferred_element_type=jnp.float32)
    state_term = state_term + lax.dot_general(
        value_grad, value_full, contract, preferred_element_type=jnp.float32
    )
    summed = lax.psum_scatter(
        state_term.astype(jnp.bfloat16), "tensor", scatter_dimension=1, tiled=True
    ).astype(jnp.float32)
    state_grad = summed.astype(jnp.bfloat16).reshape(nbr_dev, nbr_len, summed.shape[1])
    got_dq = back_dq.reshape(buffer_rows, span_len * local_width)[position]
    got_dq = got_dq.reshape(spans, neigh, span_len * local_width).astype(jnp.float32)
    query_grad = jnp.sum(got_dq, axis=1).astype(jnp.bfloat16).reshape(spans * span_len, local_width)
    return (context, query_grad, state_grad)


def solution(mesh):
    placed = (
        P("dp", "tensor"),
        P("dp", None),
        P("dp"),
        P("dp", None, None),
        P("dp", "tensor"),
        P("dp", "tensor"),
        P("dp", "tensor"),
    )
    return jax.shard_map(
        local,
        mesh=mesh,
        in_specs=placed,
        out_specs=(P("dp", "tensor"), P("dp", "tensor"), P("dp", None, "tensor")),
        check_vma=False,
    )
```

profile of v0, /device:TPU:8, one launch (start us, length us, event | category | flops | bytes accessed | tf_op | source)
XLA Modules:
  0.0 683.0 jit_solution(17984772549266577789)
XLA Ops:
  16.2 12.3 %all-to-all-start = ((bf16[64,1,64,512]{3,2,1,0:T(8,128)(2,1)}), bf16[64,1,64,512]{3,2,1,0:T(8,128)(2,1)}, u32[]{:S(2)}, u32[]{:S(2)}) async-start(bf16[64,1,64,512]{3,2,1,0:T(8,128)(2,1)} %bitcast.204), calls=%async_computation | async-start | bytes 8388608 | tf_op jit(solution)/shard_map/all_to_all | solution.py:47
  29.2 106.7 %all-to-all-done = bf16[64,1,64,512]{3,2,1,0:T(8,128)(2,1)} async-done(((bf16[64,1,64,512]{3,2,1,0:T(8,128)(2,1)}), bf16[64,1,64,512]{3,2,1,0:T(8,128)(2,1)}, u32[]{:S(2)}, u32[]{:S(2)}) %all-to-all-start) | async-done | bytes 4194336 | tf_op jit(solution)/shard_map/all_to_all | solution.py:47
  135.9 6.9 %reshape.264 = bf16[64,64,4,128]{3,2,1,0:T(4,128)(2,1)} reshape(bf16[64,1,64,512]{3,2,1,0:T(8,128)(2,1)} %all-to-all-done) | data formatting | bytes 8388608 | tf_op jit(solution)/shard_map/reshape
  142.9 5.3 copy.81
  161.8 7.0 %all-to-all-start.1 = ((f32[64,1,256]{2,1,0:T(1,128)}), f32[64,1,256]{2,1,0:T(1,128)S(1)}, u32[]{:S(2)}, u32[]{:S(2)}) async-start(f32[64,1,256]{2,1,0:T(1,128)} %reshape.325), calls=%async_computation.1 | async-start | bytes 131072 | tf_op jit(solution)/shard_map/all_to_all | solution.py:70
  168.8 6.9 %fusion.4 = bf16[64,1,64,4,128]{4,2,0,3,1:T(8,128)(2,1)} fusion(f32[64,64,4]{1,0,2:T(8,128)S(1)} %log_add_fusion, f32[4,128,4096]{1,2,0} %copy-done.2), kind=kLoop, calls=%fused_computation.15 | loop fusion | flops 6291456 | bytes 12648448 | tf_op jit(solution)/shard_map/convert_element_type | solution.py:59
  175.6 18.7 %all-gather.5.cloned.1.call-done = bf16[4096,512]{1,0:T(8,128)(2,1)} async-done(((bf16[64,512]{1,0:T(8,128)(2,1)}), bf16[4096,512]{1,0:T(8,128)(2,1)}) %all-gather.5.cloned.1.call-update) | async-done | bytes 4194320 | tf_op jit(solution)/shard_map/all_gather | solution.py:41
  203.1 14.6 %copy.86 = f32[64,1,64,4,128]{4,3,1,2,0:T(4,128)} copy(f32[64,1,64,4,128]{4,2,0,3,1:T(8,128)} %convert_bitcast_fusion) | data formatting | bytes 16777216 | tf_op jit(solution)/shard_map/convert_element_type | solution.py:68
  217.6 8.1 %convert_bitcast_fusion.1 = bf16[64,64,1,512]{3,2,1,0:T(2,128)(2,1)} fusion(f32[64,1,64,512]{3,1,2,0:T(1,128)} %bitcast.197), kind=kLoop, calls=%fused_computation.76 | loop fusion | flops 2097152 | bytes 12582912
  226.3 28.4 %reduce.4 = bf16[64,64,512]{2,1,0:T(8,128)(2,1)} reduce(bf16[64,64,1,512]{3,2,1,0:T(2,128)(2,1)} %convert_bitcast_fusion.1, bf16[]{:T(256)} %broadcast.138), dimensions={2}, to_apply=%convert_bitcast_fusion.1.reduce_sub_computation | reduce | bytes 8388610
  254.6 7.8 %reshape.323 = bf16[64,2,16384]{2,1,0:T(2,128)(2,1)} reshape(bf16[64,64,512]{2,1,0:T(8,128)(2,1)} %reduce.4) | data formatting | bytes 8388608
  262.5 8.4 %all-to-all-start.2 = ((bf16[64,2,16384]{2,1,0:T(2,128)(2,1)}), bf16[64,2,16384]{2,1,0:T(2,128)(2,1)}, u32[]{:S(2)}, u32[]{:S(2)}) async-start(bf16[64,2,16384]{2,1,0:T(2,128)(2,1)} %reshape.323), calls=%async_computation.2 | async-start | bytes 8388608 | tf_op jit(solution)/shard_map/all_to_all | solution.py:67
  278.7 88.3 %all-to-all-done.2 = bf16[64,2,16384]{2,1,0:T(2,128)(2,1)} async-done(((bf16[64,2,16384]{2,1,0:T(2,128)(2,1)}), bf16[64,2,16384]{2,1,0:T(2,128)(2,1)}, u32[]{:S(2)}, u32[]{:S(2)}) %all-to-all-start.2) | async-done | bytes 4194336 | tf_op jit(solution)/shard_map/all_to_all | solution.py:67
  367.0 19.7 %reshape.324 = bf16[64,64,1,512]{3,2,1,0:T(2,128)(2,1)} reshape(bf16[64,2,16384]{2,1,0:T(2,128)(2,1)} %all-to-all-done.2) | data formatting | bytes 8388608
  386.7 6.9 %copy.138 = bf16[64,1,64,512]{3,2,1,0:T(8,128)(2,1)} copy(bf16[64,1,64,512]{3,1,2,0:T(2,128)(2,1)} %bitcast.196) | data formatting | bytes 8388608
  397.2 5.2 multiply_convert_fusion.2
  415.3 5.8 all-to-all-start.4
  429.8 7.9 %all-to-all-start.3 = ((bf16[64,1,64,512]{3,2,1,0:T(8,128)(2,1)}), bf16[64,1,64,512]{3,2,1,0:T(8,128)(2,1)}, u32[]{:S(2)}, u32[]{:S(2)}) async-start(bf16[64,1,64,512]{3,2,1,0:T(8,128)(2,1)} %bitcast.203), calls=%async_computation.3 | async-start | bytes 8388608 | tf_op jit(solution)/shard_map/all_to_all | solution.py:102
  438.7 95.2 %all-to-all-done.3 = bf16[64,1,64,512]{3,2,1,0:T(8,128)(2,1)} async-done(((bf16[64,1,64,512]{3,2,1,0:T(8,128)(2,1)}), bf16[64,1,64,512]{3,2,1,0:T(8,128)(2,1)}, u32[]{:S(2)}, u32[]{:S(2)}) %all-to-all-start.3) | async-done | bytes 4194336 | tf_op jit(solution)/shard_map/all_to_all | solution.py:102
  533.8 6.9 %reshape.272 = bf16[64,64,4,128]{3,2,1,0:T(4,128)(2,1)} reshape(bf16[64,1,64,512]{3,2,1,0:T(8,128)(2,1)} %all-to-all-done.3) | data formatting | bytes 8388608 | tf_op jit(solution)/shard_map/reshape.6
  547.5 5.1 multiply_convert_fusion.1
  557.8 5.7 all-to-all-start.5
  577.1 82.6 %all-to-all-done.5 = bf16[64,1,64,512]{3,2,1,0:T(8,128)(2,1)} async-done(((bf16[64,1,64,512]{3,2,1,0:T(8,128)(2,1)}), bf16[64,1,64,512]{3,2,1,0:T(8,128)(2,1)}, u32[]{:S(2)}, u32[]{:S(2)}) %all-to-all-start.5) | async-done | bytes 4194336 | tf_op jit(solution)/shard_map/all_to_all | solution.py:118
  659.7 6.7 copy.110
  (112 shorter events, 101.6 us)
Async XLA Ops:
  7.2 141.0 %copy-start = (bf16[1,128,4096]{2,1,0:T(8,128)(2,1)S(1)}, bf16[1,128,4096]{2,1,0:T(8,128)(2,1)}, u32[]{:S(2)}) copy-start(bf16[1,128,4096]{2,1,0:T(8,128)(2,1)} %param.10) | copy-start | bytes 3145732
  7.2 140.9 %all-gather.3.cloned.1.call-start = ((), (), s32[]{:S(2)}) async-start(), calls=%async_computation.7 | async-start | bytes 4259840 | tf_op jit(solution)/shard_map/all_gather | solution.py:40
  8.9 3.7 copy-start.13
  16.2 119.7 %all-to-all-start = ((bf16[64,1,64,512]{3,2,1,0:T(8,128)(2,1)}), bf16[64,1,64,512]{3,2,1,0:T(8,128)(2,1)}, u32[]{:S(2)}, u32[]{:S(2)}) async-start(bf16[64,1,64,512]{3,2,1,0:T(8,128)(2,1)} %bitcast.204), calls=%async_computation | async-start | bytes 8388608 | tf_op jit(solution)/shard_map/all_to_all | solution.py:47
  28.5 165.9 %all-gather.5.cloned.1.call-start = ((), (), s32[]{:S(2)}) async-start(), calls=%async_computation.8 | async-start | bytes 4259840 | tf_op jit(solution)/shard_map/all_gather | solution.py:41
  148.1 3.5 copy-start.7
  152.9 3.2 copy-start.2
  161.8 100.7 %all-to-all-start.1 = ((f32[64,1,256]{2,1,0:T(1,128)}), f32[64,1,256]{2,1,0:T(1,128)S(1)}, u32[]{:S(2)}, u32[]{:S(2)}) async-start(f32[64,1,256]{2,1,0:T(1,128)} %reshape.325), calls=%async_computation.1 | async-start | bytes 131072 | tf_op jit(solution)/shard_map/all_to_all | solution.py:70
  194.3 3.4 copy-start.4
  262.5 8.5 %copy-start.11 = (bf16[512,512]{1,0:T(8,128)(2,1)S(1)}, bf16[512,512]{1,0:T(8,128)(2,1)}, u32[]{:S(2)}) copy-start(bf16[512,512]{1,0:T(8,128)(2,1)} %param.13) | copy-start | bytes 1572868
  262.5 9.9 %copy-start.14 = (s32[8]{0:T(128)S(1)}, s32[8]{0:T(128)}, u32[]{:S(2)}) copy-start(s32[8]{0:T(128)} %param.9) | copy-start | bytes 100
  262.5 104.5 %all-to-all-start.2 = ((bf16[64,2,16384]{2,1,0:T(2,128)(2,1)}), bf16[64,2,16384]{2,1,0:T(2,128)(2,1)}, u32[]{:S(2)}, u32[]{:S(2)}) async-start(bf16[64,2,16384]{2,1,0:T(2,128)(2,1)} %reshape.323), calls=%async_computation.2 | async-start | bytes 8388608 | tf_op jit(solution)/shard_map/all_to_all | solution.py:67
  273.0 120.6 %copy-start.12 = (s32[1024]{0:T(1024)}, s32[1024]{0:T(1024)S(1)}, u32[]{:S(2)}) copy-start(s32[1024]{0:T(1024)S(1)} %pad_clamp_fusion) | copy-start | bytes 12292
  415.3 14.6 %all-to-all-start.4 = ((f32[64,1,256]{2,1,0:T(1,128)}), f32[64,1,256]{2,1,0:T(1,128)S(1)}, u32[]{:S(2)}, u32[]{:S(2)}) async-start(f32[64,1,256]{2,1,0:T(1,128)} %reshape.327), calls=%async_computation.4 | async-start | bytes 131072 | tf_op jit(solution)/shard_map/all_to_all | solution.py:105
  429.8 104.0 %all-to-all-start.3 = ((bf16[64,1,64,512]{3,2,1,0:T(8,128)(2,1)}), bf16[64,1,64,512]{3,2,1,0:T(8,128)(2,1)}, u32[]{:S(2)}, u32[]{:S(2)}) async-start(bf16[64,1,64,512]{3,2,1,0:T(8,128)(2,1)} %bitcast.203), calls=%async_computation.3 | async-start | bytes 8388608 | tf_op jit(solution)/shard_map/all_to_all | solution.py:102
  544.1 3.4 copy-start.3
  552.6 2.0 copy-start.6
  557.8 101.9 %all-to-all-start.5 = ((bf16[64,1,64,512]{3,2,1,0:T(8,128)(2,1)}), bf16[64,1,64,512]{3,2,1,0:T(8,128)(2,1)}, u32[]{:S(2)}, u32[]{:S(2)}) async-start(bf16[64,1,64,512]{3,2,1,0:T(8,128)(2,1)} %bitcast_bitcast_fusion), calls=%async_computation.5 | async-start | bytes 8388608 | tf_op jit(solution)/shard_map/all_to_all | solution.py:118
  563.5 112.7 %reduce-scatter.2.cloned.1.call-start = ((), (), s32[]{:S(2)}) async-start(), calls=%async_computation.9 | async-start | bytes 1310720 | tf_op jit(solution)/shard_map/reduce_scatter | solution.py:133
  564.0 5.0 copy-start.9
  564.0 6.5 copy-start.10
  569.0 2.4 copy-start.5
  571.4 2.2 copy-start.8
  666.4 9.8 %copy-start.1 = (bf16[1,128,4096]{2,1,0:T(8,128)(2,1)S(1)}, bf16[1,128,4096]{2,1,0:T(8,128)(2,1)}, u32[]{:S(2)}) copy-start(bf16[1,128,4096]{2,1,0:T(8,128)(2,1)} %param.10) | copy-start | bytes 3145732
Sparse Core Ops, SparseCore 0:
  10.8 98.6 all-gather.2
  112.3 82.0 all-gather.4
  576.2 27.4 reduce-scatter.1
where the time goes:
time: 694 us; the launch traced here: 683 us
  waiting for transfers between devices  395 us (57%)
  local copies, waits for them, and re-layouts  119 us (17%)
  other arithmetic  79.9 us (12%)
  starting transfers between devices  47.5 us (7%)
  matrix products  26.4 us (4%)
  between operations  14.4 us (2%)
    all_to_all x1, waiting for transfers between devices, local(): lax.all_to_all(send_query, 'dp', split_axis=0, concat_axis=0, tiled=True)  107 us
    all_to_all x1, waiting for transfers between devices, local(): lax.all_to_all(send_grad.astype(jnp.float32), 'dp', split_axis=0, concat_...  95.2 us
    all_to_all x1, waiting for transfers between devices, local(): lax.all_to_all(item_part.astype(jnp.float32), 'dp', split_axis=0, concat_...  88.3 us
    all_to_all x1, waiting for transfers between devices, local(): lax.all_to_all(item_dq, 'dp', split_axis=0, concat_axis=0, tiled=True)  82.6 us
    unnamed x43, local copies, waits for them, and re-layouts  58.6 us
    unnamed x2, other arithmetic  36.5 us
    all_gather x1, waiting for transfers between devices, local(): value_full = lax.all_gather(w_value, 'dp', axis=0, tiled=True)  18.7 us
    convert_element_type x1, local copies, waits for them, and re-layouts, local(): item_part.astype(jnp.float32)  14.6 us
  transfers between devices with their start and end apart: 9, of which 6 were waited for; matrix products, arithmetic and copies ran while one was open for 22% of the time, Pallas kernels for 0%

commit v1 on v0

v1 whole, which is shorter than its diff:
```python
import functools
import math

import jax
import jax.numpy as jnp
from jax import lax
from jax.experimental import pallas as pl
from jax.experimental.pallas import tpu as pltpu
from jax.sharding import PartitionSpec as P

HEAD = 128
NT = (((1,), (1,)), ((), ()))
TN = (((0,), (0,)), ((), ()))


def dot(a, b, dims=(((1,), (0,)), ((), ()))):
    return lax.dot_general(a, b, dims, preferred_element_type=jnp.float32)


def span_head(q, g, k, v, live):
    scale = 1.0 / math.sqrt(HEAD)
    prob, log_total, part = [], [], []
    for j in range(2):
        s = dot(q, k[j], NT) * scale
        m = jnp.max(s, axis=-1, keepdims=True)
        e = jnp.exp(s - m)
        total = jnp.sum(e, axis=-1, keepdims=True)
        prob.append(e * (1.0 / total))
        log_total.append(m + jnp.log(total))
    half = [p.astype(jnp.bfloat16) for p in prob]
    part = [dot(half[j], v[j]).astype(jnp.bfloat16).astype(jnp.float32) for j in range(2)]
    other = jnp.where(live, log_total[1], -1e30)
    top = jnp.maximum(log_total[0], other)
    raw = [jnp.exp(log_total[0] - top), jnp.where(live, jnp.exp(other - top), 0.0)]
    norm = 1.0 / (raw[0] + raw[1])
    mix = [r * norm for r in raw]
    mixed = mix[0] * part[0] + mix[1] * part[1]
    gf = g.astype(jnp.float32)
    dq = None
    dk, dv = [], []
    for j in range(2):
        pg = (mix[j] * gf).astype(jnp.bfloat16)
        lse = mix[j] * jnp.sum(gf * (part[j] - mixed), axis=-1, keepdims=True)
        rest = jnp.sum(pg.astype(jnp.float32) * part[j], axis=-1, keepdims=True) - lse
        ds = (prob[j] * (dot(pg, v[j], NT) - rest)).astype(jnp.bfloat16)
        one = (dot(ds, k[j]) * scale).astype(jnp.bfloat16).astype(jnp.float32)
        dq = one if dq is None else dq + one
        dk.append((dot(ds, q, TN) * scale).astype(jnp.bfloat16))
        dv.append(dot(half[j], pg, TN).astype(jnp.bfloat16))
    return mixed.astype(jnp.bfloat16), dq.astype(jnp.bfloat16), dk, dv


def attend(ids, counts, q_ref, g_ref, kv_hbm, ctx_ref, dq_ref, dkv_hbm, kv, dkv, zero, named, in_sem, out_sem, zero_sem):
    slots = ids.shape[0]
    spans = slots // 2
    rows = q_ref.shape[0] // spans
    width = q_ref.shape[1]
    owners = kv_hbm.shape[0]

    def load(s):
        return pltpu.make_async_copy(kv_hbm.at[ids[s]], kv.at[s], in_sem.at[s])

    def store(s):
        return pltpu.make_async_copy(dkv.at[s], dkv_hbm.at[ids[s]], out_sem.at[s])

    for s in range(slots):
        load(s).start()
    zero[...] = jnp.zeros_like(zero)

    @pl.loop(0, owners)
    def _(n):
        named[n] = 0

    for s in range(slots):
        named[ids[s]] = 1

    @pl.loop(0, owners)
    def _(n):
        @pl.when(named[n] == 0)
        def _():
            pltpu.make_async_copy(zero, dkv_hbm.at[n], zero_sem).start()

    @pl.loop(0, spans)
    def _(c):
        load(2 * c).wait()
        load(2 * c + 1).wait()
        live = counts[c] > 1
        span = pl.ds(pl.multiple_of(c * rows, rows), rows)
        for h in range(width // HEAD):
            cols = slice(h * HEAD, (h + 1) * HEAD)
            vcols = slice(width + h * HEAD, width + (h + 1) * HEAD)
            k = [kv[2 * c + j, :, cols] for j in range(2)]
            v = [kv[2 * c + j, :, vcols] for j in range(2)]
            ctx, dq, dk, dv = span_head(q_ref[span, cols], g_ref[span, cols], k, v, live)
            ctx_ref[span, cols] = ctx
            dq_ref[span, cols] = dq
            for j in range(2):
                dkv[2 * c + j, :, cols] = dk[j]
                dkv[2 * c + j, :, vcols] = dv[j]
        store(2 * c).start()
        store(2 * c + 1).start()

    for s in range(slots):
        store(s).wait()
    rest = dkv_hbm.at[pl.ds(0, owners - slots)]
    pltpu.make_async_copy(rest, rest, zero_sem).wait()


def local(queries, neighbours, counts, states, w_key, w_value, cotangent):
    owners = lax.axis_size("dp")
    spans, neigh = neighbours.shape
    slots = spans * neigh
    tokens, width = queries.shape
    _, rows, dmodel = states.shape
    w_all = lax.all_gather(jnp.concatenate([w_key, w_value], axis=1), "dp", axis=0, tiled=True)
    kv_own = dot(states.reshape(rows, dmodel), w_all).astype(jnp.bfloat16)
    kv_all = lax.all_gather(kv_own, "dp", axis=0, tiled=False)
    vmem = pl.BlockSpec(memory_space=pltpu.VMEM)
    smem = pl.BlockSpec(memory_space=pltpu.SMEM)
    hbm = pl.BlockSpec(memory_space=pl.ANY)
    context, query_grad, dkv_all = pl.pallas_call(
        attend,
        out_shape=(
            jax.ShapeDtypeStruct((tokens, width), jnp.bfloat16),
            jax.ShapeDtypeStruct((tokens, width), jnp.bfloat16),
            jax.ShapeDtypeStruct((owners, rows, 2 * width), jnp.bfloat16),
        ),
        in_specs=[smem, smem, vmem, vmem, hbm],
        out_specs=(vmem, vmem, hbm),
        scratch_shapes=[
            pltpu.VMEM((slots, rows, 2 * width), jnp.bfloat16),
            pltpu.VMEM((slots, rows, 2 * width), jnp.bfloat16),
            pltpu.VMEM((rows, 2 * width), jnp.bfloat16),
            pltpu.SMEM((owners,), jnp.int32),
            pltpu.SemaphoreType.DMA((slots,)),
            pltpu.SemaphoreType.DMA((slots,)),
            pltpu.SemaphoreType.DMA,
        ],
        compiler_params=pltpu.CompilerParams(vmem_limit_bytes=32 << 20),
        name="attend",
    )(neighbours.reshape(slots), counts, queries, cotangent, kv_all)
    dkv = lax.psum_scatter(dkv_all.reshape(owners * rows, 2 * width), "dp", scatter_dimension=0, tiled=True)
    term = dot(dkv, w_all, NT).astype(jnp.bfloat16)
    state_grad = lax.psum_scatter(term, "tensor", scatter_dimension=1, tiled=True)
    return context, query_grad, state_grad.reshape(1, rows, state_grad.shape[1])


def solution(mesh):
    placed = (
        P("dp", "tensor"),
        P("dp", None),
        P("dp"),
        P("dp", None, None),
        P("dp", "tensor"),
        P("dp", "tensor"),
        P("dp", "tensor"),
    )
    return jax.shard_map(
        local,
        mesh=mesh,
        in_specs=placed,
        out_specs=(P("dp", "tensor"), P("dp", "tensor"), P("dp", None, "tensor")),
        check_vma=False,
    )
```

time: 694 us -> 493 us (0.71); the launches traced: 683 us -> 493 us
  local copies, waits for them, and re-layouts: 119 us -> 28.3 us
  other arithmetic: 79.9 us -> 1.61 us
  starting transfers between devices: 47.5 us -> 0.16 us
  Pallas kernels: 0 us -> 30.8 us
  matrix products: 26.4 us -> 13.8 us
  waiting for transfers between devices: 395 us -> 404 us
    all_to_all x6 -> x0, waiting for transfers between devices: 375 us -> none  [the longest x1 107 us: local(): lax.all_to_all(send_query, 'dp', split_axis=0, concat_axis=0, tiled=True)]
    reduce_scatter x1 -> x2, waiting for transfers between devices: 0.01 us -> 213 us  [the longest x1 187 us: local(): lax.psum_scatter(dkv_all.reshape(owners * rows, 2 * width), 'dp', scatter...]
    all_gather x2, waiting for transfers between devices: 18.7 us -> 191 us  [the longest x1 104 us: local(): kv_all = lax.all_gather(kv_own, 'dp', axis=0, tiled=False)]
    unnamed x43 -> x13, local copies, waits for them, and re-layouts: 58.6 us -> 5.83 us
    all_to_all x6 -> x0, starting transfers between devices: 47 us -> none  [the longest x1 12.3 us: local(): lax.all_to_all(send_query, 'dp', split_axis=0, concat_axis=0, tiled=True)]
    unnamed x2 -> x0, other arithmetic: 36.5 us -> none
    pallas_call x0 -> x1, Pallas kernels: none -> 30.8 us  [local(): pl.pallas_call(attend, out_shape=(jax.ShapeDtypeStruct((tokens, width), j...]
    all_gather x0 -> x1, local copies, waits for them, and re-layouts: none -> 22.3 us  [local(): kv_all = lax.all_gather(kv_own, 'dp', axis=0, tiled=False)]
  transfers between devices with their start and end apart: 9 -> 4, of which waited for: 6 -> 4; matrix products, arithmetic and copies ran while one was open for 22% -> 0% of each run, Pallas kernels for 0% -> 0%
where the time goes in v1:
time: 493 us
  waiting for transfers between devices  404 us (82%)
  Pallas kernels  30.8 us (6%)
  local copies, waits for them, and re-layouts  28.3 us (6%)
  matrix products  13.8 us (3%)
  between operations  13.8 us (3%)
    reduce_scatter x1, waiting for transfers between devices, local(): lax.psum_scatter(dkv_all.reshape(owners * rows, 2 * width), 'dp', scatter...  187 us
    all_gather x1, waiting for transfers between devices, local(): kv_all = lax.all_gather(kv_own, 'dp', axis=0, tiled=False)  104 us
    all_gather x1, waiting for transfers between devices, local(): lax.all_gather(jnp.concatenate([w_key, w_value], axis=1), 'dp', axis=0, t...  87.1 us
    pallas_call x1, Pallas kernels, local(): pl.pallas_call(attend, out_shape=(jax.ShapeDtypeStruct((tokens, width), j...  30.8 us
    reduce_scatter x1, waiting for transfers between devices, local(): lax.psum_scatter(term, 'tensor', scatter_dimension=1, tiled=True)  25.5 us
    all_gather x1, local copies, waits for them, and re-layouts, local(): kv_all = lax.all_gather(kv_own, 'dp', axis=0, tiled=False)  22.3 us
    dot_general x2, matrix products, dot(): return lax.dot_general(a, b, dims, preferred_element_type=jnp.float32)  13.8 us
  transfers between devices with their start and end apart: 4, of which 4 were waited for; matrix products, arithmetic and copies ran while one was open for 0% of the time, Pallas kernels for 0%

profile of v1, /device:TPU:8, one launch (start us, length us, event | category | flops | bytes accessed | tf_op | source)
XLA Modules:
  0.0 492.5 jit_solution(10103041608367939737)
XLA Ops:
  7.2 0.0 copy-start
  7.2 0.0 all-gather.4.cloned.1.call-start
  7.2 1.6 pad_maximum_fusion
  8.9 0.0 all-gather.4.cloned.1.call-update
  8.9 0.0 all-gather.6.cloned.1.call-start
  8.9 87.1 %all-gather.4.cloned.1.call-done = bf16[4096,1024]{1,0:T(8,128)(2,1)} async-done(((bf16[64,1024]{1,0:T(8,128)(2,1)}), bf16[4096,1024]{1,0:T(8,128)(2,1)}) %all-gather.4.cloned.1.call-update) | async-done | bytes 8388624 | tf_op jit(solution)/shard_map/all_gather | solution.py:115
  96.0 0.0 copy-done
  96.1 6.5 %fusion = bf16[128,1024]{0,1:T(8,128)(2,1)} fusion(bf16[4096,1024]{1,0:T(8,128)(2,1)} %all-gather.4.cloned.1.call-done, bf16[1,128,4096]{2,1,0:T(8,128)(2,1)S(1)} %copy-done), kind=kOutput, calls=%fused_computation.2 | convolution fusion | flops 1073872896 | bytes 9699328 | tf_op jit(solution)/shard_map/dot_general | solution.py:17
  102.5 0.0 all-gather.6.cloned.1.call-update
  102.5 0.0 reduce-scatter.3.cloned.1.call-start
  102.6 0.1 copy.12
  102.7 0.1 reshape.18.ids
  102.8 0.0 copy-start.4
  102.8 103.9 %all-gather.6.cloned.1.call-done = bf16[8192,1024]{0,1:T(8,128)(2,1)} async-done(((bf16[128,1024]{0,1:T(8,128)(2,1)}), bf16[8192,1024]{0,1:T(8,128)(2,1)}) %all-gather.6.cloned.1.call-update) | async-done | bytes 16777232 | tf_op jit(solution)/shard_map/all_gather | solution.py:117
  206.7 22.3 %copy.13 = bf16[8192,1024]{1,0:T(8,128)(2,1)} copy(bf16[8192,1024]{0,1:T(8,128)(2,1)} %all-gather.6.cloned.1.call-done) | data formatting | bytes 33554432 | tf_op jit(solution)/shard_map/all_gather | solution.py:117
  229.0 0.0 copy-done.3
  229.0 30.8 %attend.1 = (bf16[512,512]{1,0:T(8,128)(2,1)}, bf16[512,512]{1,0:T(8,128)(2,1)}, bf16[64,128,1024]{2,1,0:T(8,128)(2,1)S(1)}) custom-call(s32[16]{0:T(128)S(1)} %reshape.18.ids, s32[8]{0:T(128)S(1)} %copy-done.4, bf16[512,512]{1,0:T(8,128)(2,1)S(1)} %copy-done.2, bf16[512,512]{1,0:T(8,128)(2,1)S(1)} %copy-done.3, bf16[64,128,1024]{2,1,0:T(8,128)(2,1)} %bitcast.12), custom_call_target="tpu_custom_call" | custom-call | tf_op jit(solution)/shard_map/attend/pallas_call | solution.py:121
  259.9 5.7 %copy-done.1 = bf16[64,128,1024]{2,1,0:T(8,128)(2,1)} copy-done((bf16[64,128,1024]{2,1,0:T(8,128)(2,1)}, bf16[64,128,1024]{2,1,0:T(8,128)(2,1)S(1)}, u32[]{:S(2)}) %copy-start.1) | copy-done | bytes 16777240
  265.6 0.0 reduce-scatter.3.cloned.1.call-update
  265.6 0.0 reduce-scatter.5.cloned.1.call-start
  265.7 187.4 %reduce-scatter.3.cloned.1.call-done = bf16[128,1024]{1,0:T(8,128)(2,1)} async-done(((bf16[8192,1024]{1,0:T(8,128)(2,1)}), bf16[128,1024]{1,0:T(8,128)(2,1)}) %reduce-scatter.3.cloned.1.call-update) | async-done | bytes 262160 | tf_op jit(solution)/shard_map/reduce_scatter | solution.py:142
  453.1 7.3 %convolution_convert_fusion = bf16[128,4096]{1,0:T(8,128)(2,1)} fusion(bf16[128,1024]{1,0:T(8,128)(2,1)} %reduce-scatter.3.cloned.1.call-done, bf16[4096,1024]{1,0:T(8,128)(2,1)} %all-gather.4.cloned.1.call-done), kind=kOutput, calls=%fused_computation | convolution fusion | flops 1074266112 | bytes 9699328 | tf_op jit(solution)/shard_map/dot_general | solution.py:17
  460.4 0.0 reduce-scatter.5.cloned.1.call-update
  460.5 25.5 %reduce-scatter.5.cloned.1.call-done = bf16[128,1024]{1,0:T(8,128)(2,1)} async-done(((bf16[128,4096]{1,0:T(8,128)(2,1)}), bf16[128,1024]{1,0:T(8,128)(2,1)}) %reduce-scatter.5.cloned.1.call-update) | async-done | bytes 262160 | tf_op jit(solution)/shard_map/reduce_scatter | solution.py:144
  (7 shorter events, 0.0 us)
Async XLA Ops:
  7.2 88.9 %copy-start = (bf16[1,128,4096]{2,1,0:T(8,128)(2,1)S(1)}, bf16[1,128,4096]{2,1,0:T(8,128)(2,1)}, u32[]{:S(2)}) copy-start(bf16[1,128,4096]{2,1,0:T(8,128)(2,1)} %param.10) | copy-start | bytes 3145732
  7.2 95.4 %copy-start.5 = (s32[8,2]{0,1:T(2,128)S(1)}, s32[8,2]{0,1:T(2,128)}, u32[]{:S(2)}) copy-start(s32[8,2]{0,1:T(2,128)} %param.8) | copy-start | bytes 196
  7.2 88.9 %all-gather.4.cloned.1.call-start = ((), (), s32[]{:S(2)}) async-start(), calls=%async_computation.2 | async-start | bytes 8519680 | tf_op jit(solution)/shard_map/all_gather | solution.py:115
  8.9 197.8 %all-gather.6.cloned.1.call-start = ((), (), s32[]{:S(2)}) async-start(), calls=%async_computation.5 | async-start | bytes 17039360 | tf_op jit(solution)/shard_map/all_gather | solution.py:117
  102.5 350.6 %reduce-scatter.3.cloned.1.call-start = ((), (), s32[]{:S(2)}) async-start(), calls=%async_computation.3 | async-start | bytes 17039360 | tf_op jit(solution)/shard_map/reduce_scatter | solution.py:142
  102.8 126.3 %copy-start.2 = (bf16[512,512]{1,0:T(8,128)(2,1)S(1)}, bf16[512,512]{1,0:T(8,128)(2,1)}, u32[]{:S(2)}) copy-start(bf16[512,512]{1,0:T(8,128)(2,1)} %q_ref.1) | copy-start | bytes 1572868
  102.8 126.3 %copy-start.3 = (bf16[512,512]{1,0:T(8,128)(2,1)S(1)}, bf16[512,512]{1,0:T(8,128)(2,1)}, u32[]{:S(2)}) copy-start(bf16[512,512]{1,0:T(8,128)(2,1)} %g_ref.1) | copy-start | bytes 1572868
  102.8 126.3 %copy-start.4 = (s32[8]{0:T(128)S(1)}, s32[8]{0:T(128)}, u32[]{:S(2)}) copy-start(s32[8]{0:T(128)} %counts.1) | copy-start | bytes 100
  259.9 5.7 %copy-start.1 = (bf16[64,128,1024]{2,1,0:T(8,128)(2,1)}, bf16[64,128,1024]{2,1,0:T(8,128)(2,1)S(1)}, u32[]{:S(2)}) copy-start(bf16[64,128,1024]{2,1,0:T(8,128)(2,1)S(1)} %get-tuple-element.8) | copy-start | bytes 50331652
  265.6 220.4 %reduce-scatter.5.cloned.1.call-start = ((), (), s32[]{:S(2)}) async-start(), calls=%async_computation.4 | async-start | bytes 1310720 | tf_op jit(solution)/shard_map/reduce_scatter | solution.py:144
Sparse Core Ops, SparseCore 0:
  11.4 84.6 all-gather.3
  102.7 103.9 all-gather.5
  265.8 187.2 reduce-scatter.2
  460.6 25.3 reduce-scatter.4
